TPU v7x, 256 devices: a whole 4x4x8 slice. The times are simulated.
256 devices in a mesh: band: 4 (over x_hi, core), grid: 64 (over x_lo, z, y).
Axes of the slice: x: 4 (x_hi: 2, x_lo: 2; x = x_hi * 2 + x_lo), y: 4, z: 8, core: 2. Of those that a mesh axis runs over, the one named last changes fastest.
Arguments:
- orbitals: float32 [768, 16, 16, 512], P('grid', None, None, 'band'), may hold values from -24 to 24
- potential: float32 [768, 16, 16], P('grid'), may hold values from -3 to -1
- projectors: float32 [256, 8, 13, 256], P('grid'), may hold values from -0.109375 to 0.109375
- atom_planes: int32 [256, 13], P('grid'), may hold values from 0 to 23, as said below
- kb_energy: float32 [8], replicated, may hold values from 1 to 4
Outputs:
- filtered: float32 [768, 16, 16, 512], P('grid', None, None, 'band')
- correlation_gram: float32 [512, 512], P('band')
Inputs may be any that keep to these rules, and one draw needn't show every extreme that they name: `atom_planes`: each atom's row holds 13 consecutive plane numbers; the first atom starts at plane 0 and the last atom at plane 12 - 1.
All inputs are finite; a program needn't handle non-finite values.
Results may differ from a plain program's by a relative error of at most 0.0003.
Values sent between devices are 32-bit elements; how exact they have to be, the bound alone decides.
A program may use at most 128 MiB of HBM per device.

v0:
```python
import jax
import jax.numpy as jnp
from jax import lax
from jax.sharding import PartitionSpec as P

DEGREE = 4
WEIGHTS = (
    -5369.0 / 1800.0,
    12.0 / 7.0,
    -15.0 / 56.0,
    10.0 / 189.0,
    -1.0 / 112.0,
    2.0 / 1925.0,
    -1.0 / 16632.0,
)
LOWER = -4.0
CUTOFF = 1.0
UPPER = 16.0
PRECISE = lax.Precision.HIGHEST


def padded(array, sides, width):
    for axis, dim in sides:
        peers, length = (lax.axis_size(axis), array.shape[dim])
        up = [(i, (i + 1) % peers) for i in range(peers)]
        down = [(j, i) for i, j in up]
        last = lax.slice_in_dim(array, length - width, length, axis=dim)
        initial = lax.slice_in_dim(array, 0, width, axis=dim)
        before = lax.ppermute(last, axis, up)
        after = lax.ppermute(initial, axis, down)
        array = jnp.concatenate([before, array, after], axis=dim)
    return array


def shifted(array, axis, by):
    peers = lax.axis_size(axis)
    return lax.ppermute(array, axis, [(i, (i + by) % peers) for i in range(peers)])


def filter_terms(degree):
    half_span = (UPPER - CUTOFF) / 2.0
    middle = (UPPER + CUTOFF) / 2.0
    sigma_now = half_span / (LOWER - middle)
    sigma_first = sigma_now
    scales = [sigma_now / half_span]
    recall = [0.0]
    for level in range(1, degree):
        sigma_next = 1.0 / (2.0 / sigma_first - sigma_now)
        scales.append(2.0 * sigma_next / half_span)
        recall.append(sigma_now * sigma_next)
        sigma_now = sigma_next
    return (middle, scales, recall)


def second_roll(values, along):
    summed = WEIGHTS[0] * values
    for reach in range(1, 7):
        summed = summed + WEIGHTS[reach] * (
            jnp.roll(values, reach, along) + jnp.roll(values, -reach, along)
        )
    return summed


def second_planes(widened, slab_planes):
    summed = WEIGHTS[0] * widened[6 : 6 + slab_planes]
    for reach in range(1, 7):
        summed = summed + WEIGHTS[reach] * (
            widened[6 + reach : 6 + reach + slab_planes]
            + widened[6 - reach : 6 - reach + slab_planes]
        )
    return summed


def shards(orbitals, potential, projectors, atom_planes, kb_energy):
    slab_planes = orbitals.shape[0]
    orb_here = orbitals.shape[-1]
    extent = slab_planes + 12
    atom_count = atom_planes.shape[0]
    plane_marks = (
        atom_planes[:, :, None] == jnp.arange(extent, dtype=jnp.int32)[None, None, :]
    ).astype(jnp.float32)
    projector_map = jnp.einsum("abe,apbs->apes", plane_marks, projectors, precision=PRECISE)
    map_rows = atom_count * projectors.shape[1]
    projector_map = projector_map.reshape(map_rows, -1)
    energy_col = jnp.tile(kb_energy, atom_count)[:, None]
    middle, scales, recall = filter_terms(DEGREE)
    previous = orbitals
    current = orbitals
    for level in range(DEGREE):
        widened = padded(current, (("grid", 0),), 6)
        lap = (
            second_planes(widened, slab_planes) + second_roll(current, 1) + second_roll(current, 2)
        )
        local_part = -0.5 * lap + potential[..., None] * current
        correlation = (
            jnp.dot(projector_map, widened.reshape(-1, orb_here), precision=PRECISE) * energy_col
        )
        spread = lax.dot_general(
            projector_map, correlation, (((0,), (0,)), ((), ())), precision=PRECISE
        )
        spread = spread.reshape(widened.shape)
        own_part = local_part + spread[6 : 6 + slab_planes]
        low_rim = spread[:6]
        high_rim = spread[6 + slab_planes :]
        from_below = shifted(high_rim, "grid", 1)
        from_above = shifted(low_rim, "grid", -1)
        applied = own_part.at[:6].add(from_below).at[slab_planes - 6 :].add(from_above)
        result = scales[level] * (applied - middle * current)
        if level > 0:
            result = result - recall[level] * previous
        previous = current
        current = result
    flattened = current.reshape(-1, orb_here)
    piece = lax.all_gather(current, "band", axis=3, tiled=True)
    gram_part = lax.dot_general(
        flattened, piece.reshape(-1, piece.shape[-1]), (((0,), (0,)), ((), ())), precision=PRECISE
    )
    gram_total = lax.psum(gram_part, "grid")
    cell_count = slab_planes * orbitals.shape[1] * orbitals.shape[2] * lax.axis_size("grid")
    correlation_gram = gram_total * (1.0 / cell_count)
    return (current, correlation_gram)


def solution(mesh):
    return jax.shard_map(
        shards,
        mesh=mesh,
        in_specs=(
            P("grid", None, None, "band"),
            P("grid", None, None),
            P("grid", None, None, None),
            P("grid", None),
            P(),
        ),
        out_specs=(P("grid", None, None, "band"), P("band", None)),
        check_vma=False,
    )
```

profile of v0, /device:TPU:4, one launch (start us, length us, event | category | flops | bytes accessed | tf_op | source)
XLA Modules:
  0.0 995.4 jit_solution(16665948579629088824)
XLA Ops:
  7.2 2.8 fusion.325
  11.6 7.4 collective-permute-start
  60.2 5.1 fusion.326
  70.2 6.2 collective-permute-start.3
  77.7 14.2 %fusion.105 = f32[12,16,16,128]{3,2,1,0:T(8,128)S(1)} fusion(f32[12,16,16,128]{3,2,1,0:T(8,128)S(1)} %bitcast.60, f32[18,16,16,128]{3,2,1,0:T(8,128)S(1)} %get-tuple-element.305, f32[18,16,16,128]{3,2,1,0:T(8,128)S(1)} %constant_dynamic-update-slice_fusion, f32[12,15,16,128]{3,2,1,0:T(8,128)} %get-tuple-element.301, ...), kind=kLoop, calls=%fused_computation.176 | loop fusion | flops 33423360 | bytes 61353984 | tf_op jit(solution)/shard_map/add | solution.py:102
  126.6 6.4 collective-permute-start.4
  137.7 11.2 %collective-permute-done.5 = f32[6,16,16,128]{3,2,1,0:T(8,128)S(1)} collective-permute-done((f32[6,16,16,128]{3,2,1,0:T(8,128)S(1)}, f32[6,16,16,128]{3,2,1,0:T(8,128)S(1)}, u32[]{:S(2)}, u32[]{:S(2)}) %collective-permute-start.5) | collective-permute-done | bytes 786464 | tf_op jit(solution)/shard_map/ppermute | solution.py:29
  151.6 5.1 fusion.327
  159.2 6.6 collective-permute-start.7
  165.8 20.1 %fusion.71 = f32[12,16,16,128]{3,2,1,0:T(8,128)} fusion(f32[12,16,16,128]{3,2,1,0:T(8,128)} %bitcast.61, f32[12,16,16,128]{3,2,1,0:T(8,128)S(1)} %broadcast_multiply_fusion, f32[6,16,16,128]{3,2,1,0:T(8,128)S(1)} %collective-permute-done.5, f32[6,16,16,128]{3,2,1,0:T(8,128)} %copy-done.9, f32[12,15,16,128]{3,2,1,0:T(8,128)} %get-tuple-element.251, ...), kind=kLoop, calls=%fused_computation.135 | loop fusion | flops 38928384 | bytes 47198208 | tf_op jit(solution)/shard_map/add | solution.py:102
  185.9 2.4 fusion.215
  222.0 6.4 collective-permute-start.8
  233.1 9.9 collective-permute-done.9
  245.6 5.1 fusion.328
  252.1 6.4 collective-permute-start.11
  258.6 19.8 %fusion.40 = f32[12,16,16,128]{3,2,1,0:T(8,128)} fusion(f32[12,16,16,128]{3,2,1,0:T(8,128)S(1)} %bitcast.62, f32[12,16,16,128]{3,2,1,0:T(8,128)S(1)} %multiply_subtract_fusion.2, f32[6,16,16,128]{3,2,1,0:T(8,128)S(1)} %collective-permute-done.9, f32[6,16,16,128]{3,2,1,0:T(8,128)} %copy-done.11, f32[12,15,16,128]{3,2,1,0:T(8,128)} %get-tuple-element.201, ...), kind=kLoop, calls=%fused_computation.104 | loop fusion | flops 38141952 | bytes 44052480 | tf_op jit(solution)/shard_map/add | solution.py:102
  315.2 6.6 collective-permute-start.12
  326.6 8.2 collective-permute-done.13
  337.4 5.1 fusion.329
  343.9 6.5 collective-permute-start.15
  350.4 18.8 %fusion.9 = f32[12,16,16,128]{3,2,1,0:T(8,128)S(1)} fusion(f32[12,16,16,128]{3,2,1,0:T(8,128)S(1)} %bitcast.63, f32[12,16,16,128]{3,2,1,0:T(8,128)S(1)} %multiply_subtract_fusion.1, f32[6,16,16,128]{3,2,1,0:T(8,128)S(1)} %collective-permute-done.13, f32[6,16,16,128]{3,2,1,0:T(8,128)} %copy-done.10, f32[12,15,16,128]{3,2,1,0:T(8,128)} %get-tuple-element.151, ...), kind=kLoop, calls=%fused_computation.73 | loop fusion | flops 38141952 | bytes 44052480 | tf_op jit(solution)/shard_map/add | solution.py:102
  373.4 45.7 %all-gather.2.cloned.1.call-done = f32[12,16,16,512]{3,2,1,0:T(8,128)} async-done(((f32[12,16,16,128]{3,2,1,0:T(8,128)}), f32[12,16,16,512]{3,2,1,0:T(8,128)}) %all-gather.2.cloned.1.call-update) | async-done | bytes 6291472 | tf_op jit(solution)/shard_map/all_gather | solution.py:114
  419.2 7.4 convolution_bitcast_fusion.1
  426.6 560.1 %all-reduce.2.cloned.1.call-done = f32[128,512]{1,0:T(8,128)} async-done(((f32[128,512]{1,0:T(8,128)}), f32[128,512]{1,0:T(8,128)}) %all-reduce.2.cloned.1.call-update) | async-done | bytes 262160 | tf_op jit(solution)/shard_map/psum | solution.py:118
  (195 shorter events, 187.4 us)
Async XLA Ops:
  7.2 42.1 %copy-start = (f32[4,8,13,256]{3,1,2,0:T(8,128)S(1)}, f32[4,8,13,256]{3,1,2,0:T(8,128)}, u32[]{:S(2)}) copy-start(f32[4,8,13,256]{3,1,2,0:T(8,128)} %param.23) | copy-start | bytes 1277956
  7.2 11.8 %copy-start.2 = (f32[12,16,16,128]{3,2,1,0:T(8,128)S(1)}, f32[12,16,16,128]{3,2,1,0:T(8,128)}, u32[]{:S(2)}) copy-start(f32[12,16,16,128]{3,2,1,0:T(8,128)} %param.21) | copy-start | bytes 4718596
  7.2 412.0 %all-gather.2.cloned.1.call-start = ((), (), s32[]{:S(2)}) async-start(), calls=%async_computation | async-start | bytes 7864320 | tf_op jit(solution)/shard_map/all_gather | solution.py:114
  10.0 46.8 %collective-permute-start.1 = (f32[6,16,16,128]{3,2,1,0:T(8,128)}, f32[6,16,16,128]{3,2,1,0:T(8,128)}, u32[]{:S(2)}, u32[]{:S(2)}) collective-permute-start(f32[6,16,16,128]{3,2,1,0:T(8,128)} %get-tuple-element.306), channel_id=1, source_target_pairs={{0,1},{1,2},{2,3},{3,4},{4,5},{5,6},{6,7},{7,8},{8,9},{9,10},{10,1... | collective-permute-start | bytes 2359304 | tf_op jit(solution)/shard_map/ppermute | solution.py:29
  11.6 45.2 %collective-permute-start = (f32[6,16,16,128]{3,2,1,0:T(8,128)}, f32[6,16,16,128]{3,2,1,0:T(8,128)}, u32[]{:S(2)}, u32[]{:S(2)}) collective-permute-start(f32[6,16,16,128]{3,2,1,0:T(8,128)} %get-tuple-element.307), channel_id=1, source_target_pairs={{1,0},{2,1},{3,2},{4,3},{5,4},{6,5},{7,6},{8,7},{9,8},{10,9},{11,1... | collective-permute-start | bytes 2359304 | tf_op jit(solution)/shard_map/ppermute | solution.py:30
  68.3 9.3 copy-start.12
  68.3 9.3 copy-start.13
  70.1 23.6 %collective-permute-start.2 = (f32[6,16,16,128]{3,2,1,0:T(8,128)}, f32[6,16,16,128]{3,2,1,0:T(8,128)}, u32[]{:S(2)}, u32[]{:S(2)}) collective-permute-start(f32[6,16,16,128]{3,2,1,0:T(8,128)} %bitcast.5), channel_id=1, source_target_pairs={{0,1},{1,2},{2,3},{3,4},{4,5},{5,6},{6,7},{7,8},{8,9},{9,10},{10,1... | collective-permute-start | bytes 2359304 | tf_op jit(solution)/shard_map/ppermute | solution.py:37
  70.2 24.9 %collective-permute-start.3 = (f32[6,16,16,128]{3,2,1,0:T(8,128)}, f32[6,16,16,128]{3,2,1,0:T(8,128)}, u32[]{:S(2)}, u32[]{:S(2)}) collective-permute-start(f32[6,16,16,128]{3,2,1,0:T(8,128)} %bitcast.6), channel_id=1, source_target_pairs={{0,63},{1,0},{2,1},{3,2},{4,3},{5,4},{6,5},{7,6},{8,7},{9,8},{10,9... | collective-permute-start | bytes 2359304 | tf_op jit(solution)/shard_map/ppermute | solution.py:37
  126.6 22.4 %collective-permute-start.5 = (f32[6,16,16,128]{3,2,1,0:T(8,128)S(1)}, f32[6,16,16,128]{3,2,1,0:T(8,128)S(1)}, u32[]{:S(2)}, u32[]{:S(2)}) collective-permute-start(f32[6,16,16,128]{3,2,1,0:T(8,128)S(1)} %get-tuple-element.254), channel_id=1, source_target_pairs={{0,1},{1,2},{2,3},{3,4},{4,5},{5,6},{6,7},{7,8},{8,9},{9,10},{10,1... | collective-permute-start | bytes 2359304 | tf_op jit(solution)/shard_map/ppermute | solution.py:29
  126.6 22.4 %collective-permute-start.4 = (f32[6,16,16,128]{3,2,1,0:T(8,128)S(1)}, f32[6,16,16,128]{3,2,1,0:T(8,128)S(1)}, u32[]{:S(2)}, u32[]{:S(2)}) collective-permute-start(f32[6,16,16,128]{3,2,1,0:T(8,128)S(1)} %get-tuple-element.255), channel_id=1, source_target_pairs={{1,0},{2,1},{3,2},{4,3},{5,4},{6,5},{7,6},{8,7},{9,8},{10,9},{11,1... | collective-permute-start | bytes 2359304 | tf_op jit(solution)/shard_map/ppermute | solution.py:30
  159.2 26.7 %collective-permute-start.6 = (f32[6,16,16,128]{3,2,1,0:T(8,128)}, f32[6,16,16,128]{3,2,1,0:T(8,128)}, u32[]{:S(2)}, u32[]{:S(2)}) collective-permute-start(f32[6,16,16,128]{3,2,1,0:T(8,128)} %bitcast.9), channel_id=1, source_target_pairs={{0,1},{1,2},{2,3},{3,4},{4,5},{5,6},{6,7},{7,8},{8,9},{9,10},{10,1... | collective-permute-start | bytes 2359304 | tf_op jit(solution)/shard_map/ppermute | solution.py:37
  159.2 29.1 %collective-permute-start.7 = (f32[6,16,16,128]{3,2,1,0:T(8,128)}, f32[6,16,16,128]{3,2,1,0:T(8,128)}, u32[]{:S(2)}, u32[]{:S(2)}) collective-permute-start(f32[6,16,16,128]{3,2,1,0:T(8,128)} %bitcast.10), channel_id=1, source_target_pairs={{0,63},{1,0},{2,1},{3,2},{4,3},{5,4},{6,5},{7,6},{8,7},{9,8},{10,9... | collective-permute-start | bytes 2359304 | tf_op jit(solution)/shard_map/ppermute | solution.py:37
  222.0 20.9 %collective-permute-start.9 = (f32[6,16,16,128]{3,2,1,0:T(8,128)S(1)}, f32[6,16,16,128]{3,2,1,0:T(8,128)S(1)}, u32[]{:S(2)}, u32[]{:S(2)}) collective-permute-start(f32[6,16,16,128]{3,2,1,0:T(8,128)S(1)} %get-tuple-element.204), channel_id=1, source_target_pairs={{0,1},{1,2},{2,3},{3,4},{4,5},{5,6},{6,7},{7,8},{8,9},{9,10},{10,1... | collective-permute-start | bytes 2359304 | tf_op jit(solution)/shard_map/ppermute | solution.py:29
  222.0 20.9 %collective-permute-start.8 = (f32[6,16,16,128]{3,2,1,0:T(8,128)S(1)}, f32[6,16,16,128]{3,2,1,0:T(8,128)S(1)}, u32[]{:S(2)}, u32[]{:S(2)}) collective-permute-start(f32[6,16,16,128]{3,2,1,0:T(8,128)S(1)} %get-tuple-element.205), channel_id=1, source_target_pairs={{1,0},{2,1},{3,2},{4,3},{5,4},{6,5},{7,6},{8,7},{9,8},{10,9},{11,1... | collective-permute-start | bytes 2359304 | tf_op jit(solution)/shard_map/ppermute | solution.py:30
  252.1 26.2 %collective-permute-start.10 = (f32[6,16,16,128]{3,2,1,0:T(8,128)}, f32[6,16,16,128]{3,2,1,0:T(8,128)}, u32[]{:S(2)}, u32[]{:S(2)}) collective-permute-start(f32[6,16,16,128]{3,2,1,0:T(8,128)} %bitcast.13), channel_id=1, source_target_pairs={{0,1},{1,2},{2,3},{3,4},{4,5},{5,6},{6,7},{7,8},{8,9},{9,10},{10,1... | collective-permute-start | bytes 2359304 | tf_op jit(solution)/shard_map/ppermute | solution.py:37
  252.1 28.6 %collective-permute-start.11 = (f32[6,16,16,128]{3,2,1,0:T(8,128)}, f32[6,16,16,128]{3,2,1,0:T(8,128)}, u32[]{:S(2)}, u32[]{:S(2)}) collective-permute-start(f32[6,16,16,128]{3,2,1,0:T(8,128)} %bitcast.14), channel_id=1, source_target_pairs={{0,63},{1,0},{2,1},{3,2},{4,3},{5,4},{6,5},{7,6},{8,7},{9,8},{10,9... | collective-permute-start | bytes 2359304 | tf_op jit(solution)/shard_map/ppermute | solution.py:37
  315.2 19.5 %collective-permute-start.13 = (f32[6,16,16,128]{3,2,1,0:T(8,128)S(1)}, f32[6,16,16,128]{3,2,1,0:T(8,128)S(1)}, u32[]{:S(2)}, u32[]{:S(2)}) collective-permute-start(f32[6,16,16,128]{3,2,1,0:T(8,128)S(1)} %get-tuple-element.154), channel_id=1, source_target_pairs={{0,1},{1,2},{2,3},{3,4},{4,5},{5,6},{6,7},{7,8},{8,9},{9,10},{10,1... | collective-permute-start | bytes 2359304 | tf_op jit(solution)/shard_map/ppermute | solution.py:29
  315.2 19.5 %collective-permute-start.12 = (f32[6,16,16,128]{3,2,1,0:T(8,128)S(1)}, f32[6,16,16,128]{3,2,1,0:T(8,128)S(1)}, u32[]{:S(2)}, u32[]{:S(2)}) collective-permute-start(f32[6,16,16,128]{3,2,1,0:T(8,128)S(1)} %get-tuple-element.155), channel_id=1, source_target_pairs={{1,0},{2,1},{3,2},{4,3},{5,4},{6,5},{7,6},{8,7},{9,8},{10,9},{11,1... | collective-permute-start | bytes 2359304 | tf_op jit(solution)/shard_map/ppermute | solution.py:30
  343.9 25.3 %collective-permute-start.14 = (f32[6,16,16,128]{3,2,1,0:T(8,128)}, f32[6,16,16,128]{3,2,1,0:T(8,128)}, u32[]{:S(2)}, u32[]{:S(2)}) collective-permute-start(f32[6,16,16,128]{3,2,1,0:T(8,128)} %bitcast.17), channel_id=1, source_target_pairs={{0,1},{1,2},{2,3},{3,4},{4,5},{5,6},{6,7},{7,8},{8,9},{9,10},{10,1... | collective-permute-start | bytes 2359304 | tf_op jit(solution)/shard_map/ppermute | solution.py:37
  343.9 26.7 %collective-permute-start.15 = (f32[6,16,16,128]{3,2,1,0:T(8,128)}, f32[6,16,16,128]{3,2,1,0:T(8,128)}, u32[]{:S(2)}, u32[]{:S(2)}) collective-permute-start(f32[6,16,16,128]{3,2,1,0:T(8,128)} %bitcast.18), channel_id=1, source_target_pairs={{0,63},{1,0},{2,1},{3,2},{4,3},{5,4},{6,5},{7,6},{8,7},{9,8},{10,9... | collective-permute-start | bytes 2359304 | tf_op jit(solution)/shard_map/ppermute | solution.py:37
  373.4 45.8 %copy-start.3 = (f32[12,16,16,128]{3,2,1,0:T(8,128)S(1)}, f32[12,16,16,128]{3,2,1,0:T(8,128)}, u32[]{:S(2)}) copy-start(f32[12,16,16,128]{3,2,1,0:T(8,128)} %multiply_subtract_fusion) | copy-start | bytes 4718596
  373.4 613.3 %all-reduce.2.cloned.1.call-start = ((), (), s32[]{:S(2)}) async-start(), calls=%async_computation.1 | async-start | bytes 524288 | tf_op jit(solution)/shard_map/psum | solution.py:118
  419.2 569.2 %copy-start.1 = (f32[4,8,13,256]{3,1,2,0:T(8,128)S(1)}, f32[4,8,13,256]{3,1,2,0:T(8,128)}, u32[]{:S(2)}) copy-start(f32[4,8,13,256]{3,1,2,0:T(8,128)} %param.23) | copy-start | bytes 1277956
  (12 other events, 53.9 us)
Sparse Core Ops, SparseCore 0:
  373.5 45.6 all-gather.1
  426.7 559.9 all-reduce.1
where the time goes:
time: 1010 us; the launch traced here: 995 us
  waiting for transfers between devices  637 us (63%)
  local copies, waits for them, and re-layouts  155 us (15%)
  other arithmetic  98.3 us (10%)
  starting transfers between devices  54.4 us (5%)
  matrix products  36.1 us (4%)
  between operations  14.6 us (1%)
    psum x1, waiting for transfers between devices, shards(): gram_total = lax.psum(gram_part, 'grid')  560 us
    slice x96, local copies, waits for them, and re-layouts, second_roll(): jnp.roll(values, -reach, along)  137 us
    add x4, other arithmetic, shards(): own_part = local_part + spread[6:6 + slab_planes]  72.9 us
    all_gather x1, waiting for transfers between devices, shards(): piece = lax.all_gather(current, 'band', axis=3, tiled=True)  45.7 us
    ppermute x4, waiting for transfers between devices, padded(): before = lax.ppermute(last, axis, up)  29.3 us
    ppermute x4, starting transfers between devices, padded(): after = lax.ppermute(initial, axis, down)  26.8 us
    ppermute x8, starting transfers between devices, shifted(): lax.ppermute(array, axis, [(i, (i + by) % peers) for i in range(peers)])  25.9 us
    dot_general x4, matrix products, shards(): lax.dot_general(projector_map, correlation, (((0,), (0,)), ((), ())), pre...  20.3 us
  transfers between devices with their start and end apart: 18, of which 6 were waited for; matrix products, arithmetic and copies ran while one was open for 13% of the time, Pallas kernels for 0%

commit v1 on v0

--- a/solution.py
+++ b/solution.py
@@ -115,7 +115,8 @@
     gram_part = lax.dot_general(
         flattened, piece.reshape(-1, piece.shape[-1]), (((0,), (0,)), ((), ())), precision=PRECISE
     )
-    gram_total = lax.psum(gram_part, "grid")
+    lay_threads = lambda arr: lax.all_gather(arr, "grid").sum(axis=0)
+    gram_total = lay_threads(gram_part)
     cell_count = slab_planes * orbitals.shape[1] * orbitals.shape[2] * lax.axis_size("grid")
     correlation_gram = gram_total * (1.0 / cell_count)
     return (current, correlation_gram)

time: 1010 us -> 781 us (0.77)
  waiting for transfers between devices: 637 us -> 406 us
    psum x1 -> x0, waiting for transfers between devices: 560 us -> none  [shards(): gram_total = lax.psum(gram_part, 'grid')]
    all_gather x0 -> x1, waiting for transfers between devices: none -> 329 us  [shards(): lay_threads = lambda arr: lax.all_gather(arr, 'grid').sum(axis=0)]
  transfers between devices with their start and end apart: 18 -> 18, of which waited for: 6 -> 6; matrix products, arithmetic and copies ran while one was open for 13% -> 17% of each run, Pallas kernels for 0% -> 0%
where the time goes in v1:
time: 781 us; the launch traced here: 771 us
  waiting for transfers between devices  406 us (52%)
  local copies, waits for them, and re-layouts  155 us (20%)
  other arithmetic  105 us (13%)
  starting transfers between devices  54.4 us (7%)
  matrix products  36.1 us (5%)
  between operations  14.6 us (2%)
    all_gather x1, waiting for transfers between devices, shards(): lay_threads = lambda arr: lax.all_gather(arr, 'grid').sum(axis=0)  329 us
    slice x96, local copies, waits for them, and re-layouts, second_roll(): jnp.roll(values, -reach, along)  137 us
    add x4, other arithmetic, shards(): own_part = local_part + spread[6:6 + slab_planes]  72.9 us
    all_gather x1, waiting for transfers between devices, shards(): piece = lax.all_gather(current, 'band', axis=3, tiled=True)  45.7 us
    ppermute x4, waiting for transfers between devices, padded(): before = lax.ppermute(last, axis, up)  29.3 us
    ppermute x4, starting transfers between devices, padded(): after = lax.ppermute(initial, axis, down)  26.8 us
    ppermute x8, starting transfers between devices, shifted(): lax.ppermute(array, axis, [(i, (i + by) % peers) for i in range(peers)])  25.9 us
    dot_general x4, matrix products, shards(): lax.dot_general(projector_map, correlation, (((0,), (0,)), ((), ())), pre...  20.3 us
  transfers between devices with their start and end apart: 18, of which 6 were waited for; matrix products, arithmetic and copies ran while one was open for 17% of the time, Pallas kernels for 0%

profile of v1, /device:TPU:4, one launch (start us, length us, event | category | flops | bytes accessed | tf_op | source)
XLA Modules:
  0.0 771.0 jit_solution(2904608791884800853)
XLA Ops:
  7.2 2.8 fusion.325
  11.6 7.4 collective-permute-start
  60.2 5.1 fusion.326
  70.2 6.2 collective-permute-start.3
  77.7 14.2 %fusion.105 = f32[12,16,16,128]{3,2,1,0:T(8,128)S(1)} fusion(f32[12,16,16,128]{3,2,1,0:T(8,128)S(1)} %bitcast.62, f32[18,16,16,128]{3,2,1,0:T(8,128)S(1)} %get-tuple-element.305, f32[18,16,16,128]{3,2,1,0:T(8,128)S(1)} %constant_dynamic-update-slice_fusion, f32[12,15,16,128]{3,2,1,0:T(8,128)} %get-tuple-element.301, ...), kind=kLoop, calls=%fused_computation.176 | loop fusion | flops 33423360 | bytes 61353984 | tf_op jit(solution)/shard_map/add | solution.py:102
  126.6 6.4 collective-permute-start.4
  137.7 11.2 %collective-permute-done.5 = f32[6,16,16,128]{3,2,1,0:T(8,128)S(1)} collective-permute-done((f32[6,16,16,128]{3,2,1,0:T(8,128)S(1)}, f32[6,16,16,128]{3,2,1,0:T(8,128)S(1)}, u32[]{:S(2)}, u32[]{:S(2)}) %collective-permute-start.5) | collective-permute-done | bytes 786464 | tf_op jit(solution)/shard_map/ppermute | solution.py:29
  151.6 5.1 fusion.327
  159.2 6.6 collective-permute-start.7
  165.8 20.1 %fusion.71 = f32[12,16,16,128]{3,2,1,0:T(8,128)} fusion(f32[12,16,16,128]{3,2,1,0:T(8,128)} %bitcast.63, f32[12,16,16,128]{3,2,1,0:T(8,128)S(1)} %broadcast_multiply_fusion, f32[6,16,16,128]{3,2,1,0:T(8,128)S(1)} %collective-permute-done.5, f32[6,16,16,128]{3,2,1,0:T(8,128)} %copy-done.9, f32[12,15,16,128]{3,2,1,0:T(8,128)} %get-tuple-element.251, ...), kind=kLoop, calls=%fused_computation.135 | loop fusion | flops 38928384 | bytes 47198208 | tf_op jit(solution)/shard_map/add | solution.py:102
  222.0 6.4 collective-permute-start.8
  233.1 9.9 %collective-permute-done.9 = f32[6,16,16,128]{3,2,1,0:T(8,128)S(1)} collective-permute-done((f32[6,16,16,128]{3,2,1,0:T(8,128)S(1)}, f32[6,16,16,128]{3,2,1,0:T(8,128)S(1)}, u32[]{:S(2)}, u32[]{:S(2)}) %collective-permute-start.9) | collective-permute-done | bytes 786464 | tf_op jit(solution)/shard_map/ppermute | solution.py:29
  245.6 5.1 fusion.328
  252.1 6.4 collective-permute-start.11
  258.6 19.8 %fusion.40 = f32[12,16,16,128]{3,2,1,0:T(8,128)} fusion(f32[12,16,16,128]{3,2,1,0:T(8,128)S(1)} %bitcast.64, f32[12,16,16,128]{3,2,1,0:T(8,128)S(1)} %multiply_subtract_fusion.2, f32[6,16,16,128]{3,2,1,0:T(8,128)S(1)} %collective-permute-done.9, f32[6,16,16,128]{3,2,1,0:T(8,128)} %copy-done.11, f32[12,15,16,128]{3,2,1,0:T(8,128)} %get-tuple-element.201, ...), kind=kLoop, calls=%fused_computation.104 | loop fusion | flops 38141952 | bytes 44052480 | tf_op jit(solution)/shard_map/add | solution.py:102
  315.2 6.6 collective-permute-start.12
  326.6 8.2 %collective-permute-done.13 = f32[6,16,16,128]{3,2,1,0:T(8,128)S(1)} collective-permute-done((f32[6,16,16,128]{3,2,1,0:T(8,128)S(1)}, f32[6,16,16,128]{3,2,1,0:T(8,128)S(1)}, u32[]{:S(2)}, u32[]{:S(2)}) %collective-permute-start.13) | collective-permute-done | bytes 786464 | tf_op jit(solution)/shard_map/ppermute | solution.py:29
  337.4 5.1 fusion.329
  343.9 6.5 collective-permute-start.15
  350.4 18.8 %fusion.9 = f32[12,16,16,128]{3,2,1,0:T(8,128)S(1)} fusion(f32[12,16,16,128]{3,2,1,0:T(8,128)S(1)} %bitcast.65, f32[12,16,16,128]{3,2,1,0:T(8,128)S(1)} %multiply_subtract_fusion.1, f32[6,16,16,128]{3,2,1,0:T(8,128)S(1)} %collective-permute-done.13, f32[6,16,16,128]{3,2,1,0:T(8,128)} %copy-done.10, f32[12,15,16,128]{3,2,1,0:T(8,128)} %get-tuple-element.151, ...), kind=kLoop, calls=%fused_computation.73 | loop fusion | flops 38141952 | bytes 44052480 | tf_op jit(solution)/shard_map/add | solution.py:102
  373.4 45.7 %all-gather.4.cloned.1.call-done = f32[12,16,16,512]{3,2,1,0:T(8,128)} async-done(((f32[12,16,16,128]{3,2,1,0:T(8,128)}), f32[12,16,16,512]{3,2,1,0:T(8,128)}) %all-gather.4.cloned.1.call-update) | async-done | bytes 6291472 | tf_op jit(solution)/shard_map/all_gather | solution.py:114
  419.2 7.3 convolution_bitcast_fusion.1
  426.5 329.2 %all-gather.6.cloned.1.call-done = f32[8192,512]{1,0:T(8,128)} async-done(((f32[128,512]{1,0:T(8,128)}), f32[8192,512]{1,0:T(8,128)}) %all-gather.6.cloned.1.call-update) | async-done | bytes 16777232 | tf_op jit(solution)/shard_map/all_gather | solution.py:118
  755.7 7.6 reduce_sum.9
  (196 shorter events, 188.8 us)
Async XLA Ops:
  7.2 42.1 %copy-start = (f32[4,8,13,256]{3,1,2,0:T(8,128)S(1)}, f32[4,8,13,256]{3,1,2,0:T(8,128)}, u32[]{:S(2)}) copy-start(f32[4,8,13,256]{3,1,2,0:T(8,128)} %param.23) | copy-start | bytes 1277956
  7.2 11.8 %copy-start.2 = (f32[12,16,16,128]{3,2,1,0:T(8,128)S(1)}, f32[12,16,16,128]{3,2,1,0:T(8,128)}, u32[]{:S(2)}) copy-start(f32[12,16,16,128]{3,2,1,0:T(8,128)} %param.21) | copy-start | bytes 4718596
  7.2 412.0 %all-gather.4.cloned.1.call-start = ((), (), s32[]{:S(2)}) async-start(), calls=%async_computation | async-start | bytes 7864320 | tf_op jit(solution)/shard_map/all_gather | solution.py:114
  10.0 46.8 %collective-permute-start.1 = (f32[6,16,16,128]{3,2,1,0:T(8,128)}, f32[6,16,16,128]{3,2,1,0:T(8,128)}, u32[]{:S(2)}, u32[]{:S(2)}) collective-permute-start(f32[6,16,16,128]{3,2,1,0:T(8,128)} %get-tuple-element.306), channel_id=1, source_target_pairs={{0,1},{1,2},{2,3},{3,4},{4,5},{5,6},{6,7},{7,8},{8,9},{9,10},{10,1... | collective-permute-start | bytes 2359304 | tf_op jit(solution)/shard_map/ppermute | solution.py:29
  11.6 45.2 %collective-permute-start = (f32[6,16,16,128]{3,2,1,0:T(8,128)}, f32[6,16,16,128]{3,2,1,0:T(8,128)}, u32[]{:S(2)}, u32[]{:S(2)}) collective-permute-start(f32[6,16,16,128]{3,2,1,0:T(8,128)} %get-tuple-element.307), channel_id=1, source_target_pairs={{1,0},{2,1},{3,2},{4,3},{5,4},{6,5},{7,6},{8,7},{9,8},{10,9},{11,1... | collective-permute-start | bytes 2359304 | tf_op jit(solution)/shard_map/ppermute | solution.py:30
  68.3 9.3 %copy-start.12 = (f32[12,16,5,128]{3,2,1,0:T(8,128)S(1)}, f32[12,16,5,128]{3,2,1,0:T(8,128)}, u32[]{:S(2)}) copy-start(f32[12,16,5,128]{3,2,1,0:T(8,128)} %get-tuple-element.262) | copy-start | bytes 1474564
  68.3 9.3 %copy-start.13 = (f32[12,16,3,128]{3,2,1,0:T(4,128)S(1)}, f32[12,16,3,128]{3,2,1,0:T(4,128)}, u32[]{:S(2)}) copy-start(f32[12,16,3,128]{3,2,1,0:T(4,128)} %get-tuple-element.270) | copy-start | bytes 884740
  70.1 23.6 %collective-permute-start.2 = (f32[6,16,16,128]{3,2,1,0:T(8,128)}, f32[6,16,16,128]{3,2,1,0:T(8,128)}, u32[]{:S(2)}, u32[]{:S(2)}) collective-permute-start(f32[6,16,16,128]{3,2,1,0:T(8,128)} %bitcast.5), channel_id=1, source_target_pairs={{0,1},{1,2},{2,3},{3,4},{4,5},{5,6},{6,7},{7,8},{8,9},{9,10},{10,1... | collective-permute-start | bytes 2359304 | tf_op jit(solution)/shard_map/ppermute | solution.py:37
  70.2 24.9 %collective-permute-start.3 = (f32[6,16,16,128]{3,2,1,0:T(8,128)}, f32[6,16,16,128]{3,2,1,0:T(8,128)}, u32[]{:S(2)}, u32[]{:S(2)}) collective-permute-start(f32[6,16,16,128]{3,2,1,0:T(8,128)} %bitcast.6), channel_id=1, source_target_pairs={{0,63},{1,0},{2,1},{3,2},{4,3},{5,4},{6,5},{7,6},{8,7},{9,8},{10,9... | collective-permute-start | bytes 2359304 | tf_op jit(solution)/shard_map/ppermute | solution.py:37
  126.6 22.4 %collective-permute-start.5 = (f32[6,16,16,128]{3,2,1,0:T(8,128)S(1)}, f32[6,16,16,128]{3,2,1,0:T(8,128)S(1)}, u32[]{:S(2)}, u32[]{:S(2)}) collective-permute-start(f32[6,16,16,128]{3,2,1,0:T(8,128)S(1)} %get-tuple-element.254), channel_id=1, source_target_pairs={{0,1},{1,2},{2,3},{3,4},{4,5},{5,6},{6,7},{7,8},{8,9},{9,10},{10,1... | collective-permute-start | bytes 2359304 | tf_op jit(solution)/shard_map/ppermute | solution.py:29
  126.6 22.4 %collective-permute-start.4 = (f32[6,16,16,128]{3,2,1,0:T(8,128)S(1)}, f32[6,16,16,128]{3,2,1,0:T(8,128)S(1)}, u32[]{:S(2)}, u32[]{:S(2)}) collective-permute-start(f32[6,16,16,128]{3,2,1,0:T(8,128)S(1)} %get-tuple-element.255), channel_id=1, source_target_pairs={{1,0},{2,1},{3,2},{4,3},{5,4},{6,5},{7,6},{8,7},{9,8},{10,9},{11,1... | collective-permute-start | bytes 2359304 | tf_op jit(solution)/shard_map/ppermute | solution.py:30
  159.2 26.7 %collective-permute-start.6 = (f32[6,16,16,128]{3,2,1,0:T(8,128)}, f32[6,16,16,128]{3,2,1,0:T(8,128)}, u32[]{:S(2)}, u32[]{:S(2)}) collective-permute-start(f32[6,16,16,128]{3,2,1,0:T(8,128)} %bitcast.9), channel_id=1, source_target_pairs={{0,1},{1,2},{2,3},{3,4},{4,5},{5,6},{6,7},{7,8},{8,9},{9,10},{10,1... | collective-permute-start | bytes 2359304 | tf_op jit(solution)/shard_map/ppermute | solution.py:37
  159.2 29.1 %collective-permute-start.7 = (f32[6,16,16,128]{3,2,1,0:T(8,128)}, f32[6,16,16,128]{3,2,1,0:T(8,128)}, u32[]{:S(2)}, u32[]{:S(2)}) collective-permute-start(f32[6,16,16,128]{3,2,1,0:T(8,128)} %bitcast.10), channel_id=1, source_target_pairs={{0,63},{1,0},{2,1},{3,2},{4,3},{5,4},{6,5},{7,6},{8,7},{9,8},{10,9... | collective-permute-start | bytes 2359304 | tf_op jit(solution)/shard_map/ppermute | solution.py:37
  222.0 20.9 %collective-permute-start.9 = (f32[6,16,16,128]{3,2,1,0:T(8,128)S(1)}, f32[6,16,16,128]{3,2,1,0:T(8,128)S(1)}, u32[]{:S(2)}, u32[]{:S(2)}) collective-permute-start(f32[6,16,16,128]{3,2,1,0:T(8,128)S(1)} %get-tuple-element.204), channel_id=1, source_target_pairs={{0,1},{1,2},{2,3},{3,4},{4,5},{5,6},{6,7},{7,8},{8,9},{9,10},{10,1... | collective-permute-start | bytes 2359304 | tf_op jit(solution)/shard_map/ppermute | solution.py:29
  222.0 20.9 %collective-permute-start.8 = (f32[6,16,16,128]{3,2,1,0:T(8,128)S(1)}, f32[6,16,16,128]{3,2,1,0:T(8,128)S(1)}, u32[]{:S(2)}, u32[]{:S(2)}) collective-permute-start(f32[6,16,16,128]{3,2,1,0:T(8,128)S(1)} %get-tuple-element.205), channel_id=1, source_target_pairs={{1,0},{2,1},{3,2},{4,3},{5,4},{6,5},{7,6},{8,7},{9,8},{10,9},{11,1... | collective-permute-start | bytes 2359304 | tf_op jit(solution)/shard_map/ppermute | solution.py:30
  252.1 26.2 %collective-permute-start.10 = (f32[6,16,16,128]{3,2,1,0:T(8,128)}, f32[6,16,16,128]{3,2,1,0:T(8,128)}, u32[]{:S(2)}, u32[]{:S(2)}) collective-permute-start(f32[6,16,16,128]{3,2,1,0:T(8,128)} %bitcast.13), channel_id=1, source_target_pairs={{0,1},{1,2},{2,3},{3,4},{4,5},{5,6},{6,7},{7,8},{8,9},{9,10},{10,1... | collective-permute-start | bytes 2359304 | tf_op jit(solution)/shard_map/ppermute | solution.py:37
  252.1 28.6 %collective-permute-start.11 = (f32[6,16,16,128]{3,2,1,0:T(8,128)}, f32[6,16,16,128]{3,2,1,0:T(8,128)}, u32[]{:S(2)}, u32[]{:S(2)}) collective-permute-start(f32[6,16,16,128]{3,2,1,0:T(8,128)} %bitcast.14), channel_id=1, source_target_pairs={{0,63},{1,0},{2,1},{3,2},{4,3},{5,4},{6,5},{7,6},{8,7},{9,8},{10,9... | collective-permute-start | bytes 2359304 | tf_op jit(solution)/shard_map/ppermute | solution.py:37
  315.2 19.5 %collective-permute-start.13 = (f32[6,16,16,128]{3,2,1,0:T(8,128)S(1)}, f32[6,16,16,128]{3,2,1,0:T(8,128)S(1)}, u32[]{:S(2)}, u32[]{:S(2)}) collective-permute-start(f32[6,16,16,128]{3,2,1,0:T(8,128)S(1)} %get-tuple-element.154), channel_id=1, source_target_pairs={{0,1},{1,2},{2,3},{3,4},{4,5},{5,6},{6,7},{7,8},{8,9},{9,10},{10,1... | collective-permute-start | bytes 2359304 | tf_op jit(solution)/shard_map/ppermute | solution.py:29
  315.2 19.5 %collective-permute-start.12 = (f32[6,16,16,128]{3,2,1,0:T(8,128)S(1)}, f32[6,16,16,128]{3,2,1,0:T(8,128)S(1)}, u32[]{:S(2)}, u32[]{:S(2)}) collective-permute-start(f32[6,16,16,128]{3,2,1,0:T(8,128)S(1)} %get-tuple-element.155), channel_id=1, source_target_pairs={{1,0},{2,1},{3,2},{4,3},{5,4},{6,5},{7,6},{8,7},{9,8},{10,9},{11,1... | collective-permute-start | bytes 2359304 | tf_op jit(solution)/shard_map/ppermute | solution.py:30
  343.9 25.3 %collective-permute-start.14 = (f32[6,16,16,128]{3,2,1,0:T(8,128)}, f32[6,16,16,128]{3,2,1,0:T(8,128)}, u32[]{:S(2)}, u32[]{:S(2)}) collective-permute-start(f32[6,16,16,128]{3,2,1,0:T(8,128)} %bitcast.17), channel_id=1, source_target_pairs={{0,1},{1,2},{2,3},{3,4},{4,5},{5,6},{6,7},{7,8},{8,9},{9,10},{10,1... | collective-permute-start | bytes 2359304 | tf_op jit(solution)/shard_map/ppermute | solution.py:37
  343.9 26.7 %collective-permute-start.15 = (f32[6,16,16,128]{3,2,1,0:T(8,128)}, f32[6,16,16,128]{3,2,1,0:T(8,128)}, u32[]{:S(2)}, u32[]{:S(2)}) collective-permute-start(f32[6,16,16,128]{3,2,1,0:T(8,128)} %bitcast.18), channel_id=1, source_target_pairs={{0,63},{1,0},{2,1},{3,2},{4,3},{5,4},{6,5},{7,6},{8,7},{9,8},{10,9... | collective-permute-start | bytes 2359304 | tf_op jit(solution)/shard_map/ppermute | solution.py:37
  373.4 45.8 %copy-start.3 = (f32[12,16,16,128]{3,2,1,0:T(8,128)S(1)}, f32[12,16,16,128]{3,2,1,0:T(8,128)}, u32[]{:S(2)}) copy-start(f32[12,16,16,128]{3,2,1,0:T(8,128)} %multiply_subtract_fusion) | copy-start | bytes 4718596
  373.4 382.3 %all-gather.6.cloned.1.call-start = ((), (), s32[]{:S(2)}) async-start(), calls=%async_computation.1 | async-start | bytes 17039360 | tf_op jit(solution)/shard_map/all_gather | solution.py:118
  755.7 8.3 %copy-start.1 = (f32[4,8,13,256]{3,1,2,0:T(8,128)S(1)}, f32[4,8,13,256]{3,1,2,0:T(8,128)}, u32[]{:S(2)}) copy-start(f32[4,8,13,256]{3,1,2,0:T(8,128)} %param.23) | copy-start | bytes 1277956
  (12 other events, 53.9 us)
Sparse Core Ops, SparseCore 0:
  373.5 45.6 all-gather.3
  426.6 329.0 all-gather.5
